TPU v7x, 32 devices: a whole 2x2x4 slice. The times are simulated.
32 devices in a mesh: ty: 4 (over y, x), tx: 4 (over z), slide: 2 (over core).
Axes of the slice: x: 2, y: 2, z: 4, core: 2. Of those that a mesh axis runs over, the one named last changes fastest.
Arguments:
- tokens: bfloat16 [8, 4, 192, 768], P(('slide', 'ty'), 'tx'), parts along dimension 0, may hold values from -6 to 6
- summary: bfloat16 [512, 768], P(('slide', 'ty', 'tx')), parts along dimension 0, may hold values from -6 to 6
- counts: int32 [8, 4], P('slide'), parts along dimension 0, may hold values from 1 to 192, as said below
- tile_pattern: int32 [8, 4, 9], P('slide'), parts along dimension 0, may hold values from 0 to 1, as said below
- summary_pattern: int32 [8, 4, 2], P(('slide', 'ty'), 'tx'), parts along dimension 0, may hold values 0 or 1
- norm_gain: float32 [768], replicated, may hold values from 0.1 to 1.9
- projections: bfloat16 [4, 768, 768], replicated, may hold values from -4 to 4
- cotangent: bfloat16 [8, 4, 192, 768], P(('slide', 'ty'), 'tx'), parts along dimension 0, may hold values from -6 to 6
Outputs:
- updated: bfloat16 [8, 4, 192, 768], P(('slide', 'ty'), 'tx'), parts along dimension 0
- grad_tokens: bfloat16 [8, 4, 192, 768], P(('slide', 'ty'), 'tx'), parts along dimension 0
- grad_summary: bfloat16 [512, 768], P(('slide', 'ty', 'tx')), parts along dimension 0
- grad_proj: float32 [8, 768, 768], P('slide'), parts along dimension 0
- grad_gain: float32 [1536], P('slide'), parts along dimension 0
There are 2 independent parts, one for each index of `slide`. A program takes and returns all parts, laid end to end along the dimension named above; an argument that names none is the same for every part. Nothing has to cross between parts.
Inputs may be any that keep to these rules, and one draw needn't show every extreme that they name: `counts`: some tile holds exactly 192 tokens and some tile exactly 1 in every draw. `tile_pattern`: entry 4, the tile itself, is always 1.
All inputs are finite; a program needn't handle non-finite values. No bound on the sum of `summary_pattern` on one device may be relied on, other than what follows from the above.
Results may differ from a plain program's by a relative error of at most 0.011.
Values may be sent and summed in bfloat16 or wider, within the bound.
No kernel may reach another device: no remote copies, remote signals or barrier semaphores. Data moves between devices by JAX's collectives and lax.ppermute only.
A program may use at most 128 MiB of HBM per device.

v0:
```python
import math
import jax
import jax.numpy as jnp
from jax import lax
from jax.sharding import PartitionSpec as P

HEADS = 12
SBLK = 128
epsilon = 1e-05


def with_halo(cells, sides, width):
    for axis, dim in sides:
        count = lax.axis_size(axis)
        ends = count - 1
        head = lax.slice_in_dim(cells, 0, width, axis=dim)
        tail = lax.slice_in_dim(cells, cells.shape[dim] - width, cells.shape[dim], axis=dim)
        cells = jnp.concatenate(
            [
                lax.ppermute(tail, axis, [(i, (i + 1) % count) for i in range(ends)]),
                cells,
                lax.ppermute(head, axis, [((i + 1) % count, i) for i in range(ends)]),
            ],
            axis=dim,
        )
    return cells


def passed_along(array, axis, by):
    peers = lax.axis_size(axis)
    pairs = [(i, i + by) for i in range(peers) if 0 <= i + by < peers]
    return lax.ppermute(array, axis, pairs)


def shortened(array):
    return jax.tree.map(lambda a: a.astype(jnp.bfloat16) if a.dtype == jnp.float32 else a, array)


def normalize(rows, gain):
    values = rows.astype(jnp.float32)
    scale = lax.rsqrt(jnp.mean(values * values, axis=-1, keepdims=True) + epsilon)
    return ((values * scale * gain).astype(jnp.bfloat16), scale)


def norm_back(rows, scale, gain, grad_norm):
    values = rows.astype(jnp.float32)
    scaled = gain * grad_norm
    return scale * scaled - values * scale**3 * jnp.mean(values * scaled, axis=-1, keepdims=True)


def project(rows, weight):
    return jnp.dot(rows, weight, preferred_element_type=jnp.float32).astype(jnp.bfloat16)


def back_project(rows, weight):
    return lax.dot_general(
        rows, weight, (((1,), (1,)), ((), ())), preferred_element_type=jnp.float32
    )


def exact_back(rows, weight):
    return lax.dot_general(
        rows, weight.astype(jnp.float32), (((1,), (1,)), ((), ())), precision=lax.Precision.HIGHEST
    )


def contract_rows(left, right):
    return lax.dot_general(
        left, right, (((0,), (0,)), ((), ())), preferred_element_type=jnp.float32
    )


def exact_rows(left, right):
    return lax.dot_general(
        left.astype(jnp.float32), right, (((0,), (0,)), ((), ())), precision=lax.Precision.HIGHEST
    )


def grouped(rows, group_width):
    return rows.reshape(rows.shape[0], -1, group_width).transpose(1, 0, 2)


def ungrouped(stacked):
    return stacked.transpose(1, 0, 2).reshape(stacked.shape[1], -1)


def head_scores(query_part, key_part, head_size, factor, allowed):
    query_heads = query_part.reshape(query_part.shape[0], -1, head_size)
    key_heads = key_part.reshape(key_part.shape[0], -1, head_size)
    scores = (
        jnp.einsum("qhd,khd->hqk", query_heads, key_heads, preferred_element_type=jnp.float32)
        * factor
    )
    return jnp.where(allowed[None, None, :], scores, -jnp.inf)


def softmax_grads(
    query_part, key_part, value_part, grad_part, log_totals, row_delta, allowed, head_size, factor
):
    scores = head_scores(query_part, key_part, head_size, factor, allowed)
    weights_full = jnp.exp(scores - log_totals[:, :, None])
    grad_heads = grad_part.reshape(grad_part.shape[0], -1, head_size)
    value_heads = value_part.reshape(value_part.shape[0], -1, head_size)
    grad_weights = jnp.einsum(
        "qhd,khd->hqk", grad_heads, value_heads, preferred_element_type=jnp.float32
    )
    row_delta = jnp.sum(weights_full * grad_weights, axis=-1)
    grad_scores = (weights_full * (grad_weights - row_delta[:, :, None])).astype(jnp.bfloat16)
    return (weights_full.astype(jnp.bfloat16), grad_scores, row_delta)


def key_side(grad_scores, weights_half, query_part, grad_part, head_size, factor):
    query_heads = query_part.reshape(query_part.shape[0], -1, head_size)
    grad_heads = grad_part.reshape(grad_part.shape[0], -1, head_size)
    key_grad = (
        jnp.einsum("hqk,qhd->khd", grad_scores, query_heads, preferred_element_type=jnp.float32)
        * factor
    )
    value_grad = jnp.einsum(
        "hqk,qhd->khd", weights_half, grad_heads, preferred_element_type=jnp.float32
    )
    return (key_grad.reshape(key_grad.shape[0], -1), value_grad.reshape(value_grad.shape[0], -1))


def local(
    tokens, summary, counts, tile_pattern, summary_pattern, norm_gain, projections, cotangent
):
    tile_rows = tokens.shape[2]
    model_width = tokens.shape[3]
    head_size = model_width // HEADS
    group_width = 2 * head_size
    factor = 1.0 / math.sqrt(head_size)
    near_rows = 9 * tile_rows
    zero = jnp.zeros((), jnp.int32)
    grid_row = lax.axis_index("ty")
    grid_col = lax.axis_index("tx")
    token_rows = tokens[0, 0]
    grads_in = cotangent[0, 0]
    w_query, w_key, w_value, w_out = (
        projections[0],
        projections[1],
        projections[2],
        projections[3],
    )
    hidden, row_scale = normalize(token_rows, norm_gain)
    summary_hidden, summary_scale = normalize(summary, norm_gain)
    queries = project(hidden, w_query)
    keys = project(hidden, w_key)
    values = project(hidden, w_value)
    piece = lax.all_gather(summary_hidden, ("ty", "tx"), axis=0, tiled=True)
    every_summary = jnp.concatenate([project(piece, w_key), project(piece, w_value)], axis=1)
    own_pair = jnp.concatenate([keys, values], axis=1).reshape(1, 1, tile_rows, 2 * model_width)
    near_pairs = with_halo(own_pair, (("ty", 0), ("tx", 1)), 1).reshape(near_rows, 2 * model_width)
    all_keys = jnp.concatenate(
        [near_pairs[:, :model_width], every_summary[:, :model_width]], axis=0
    )
    all_values = jnp.concatenate(
        [near_pairs[:, model_width:], every_summary[:, model_width:]], axis=0
    )
    count_pad = jnp.pad(counts, 1)
    near_counts = lax.dynamic_slice(count_pad, (grid_row, grid_col), (3, 3)).reshape(9)
    tile_flags = lax.dynamic_slice(tile_pattern, (grid_row, grid_col, zero), (1, 1, 9)).reshape(9)
    positions = jnp.arange(tile_rows, dtype=jnp.int32)
    tile_ok = ((positions[None, :] < near_counts[:, None]) & (tile_flags[:, None] == 1)).reshape(
        near_rows
    )
    summary_ok = jnp.repeat(summary_pattern[0, 0] == 1, SBLK)
    allowed = jnp.concatenate([tile_ok, summary_ok])
    own_valid = positions < near_counts[4]
    row_mask = own_valid.astype(jnp.float32)[:, None]
    query_groups = grouped(queries, group_width)
    key_groups = grouped(all_keys, group_width)
    value_groups = grouped(all_values, group_width)

    def forward_group(parts):
        query_part, key_part, value_part = parts
        scores = head_scores(query_part, key_part, head_size, factor, allowed)
        largest = jnp.max(scores, axis=-1, keepdims=True)
        exponent = jnp.exp(scores - largest)
        denominator = jnp.sum(exponent, axis=-1, keepdims=True)
        weights_half = (exponent / denominator).astype(jnp.bfloat16)
        value_heads = value_part.reshape(value_part.shape[0], -1, head_size)
        mixed = jnp.einsum(
            "hqk,khd->qhd", weights_half, value_heads, preferred_element_type=jnp.float32
        )
        return (
            mixed.reshape(mixed.shape[0], -1).astype(jnp.bfloat16),
            (largest + jnp.log(denominator))[:, :, 0],
        )

    attended_groups, log_totals = lax.map(forward_group, (query_groups, key_groups, value_groups))
    attended = ungrouped(attended_groups)
    mixed_rows = jnp.dot(attended, w_out, preferred_element_type=jnp.float32)
    updated = (token_rows.astype(jnp.float32) + row_mask * mixed_rows).astype(jnp.bfloat16)
    masked = grads_in * row_mask.astype(jnp.bfloat16)
    attended_grad = back_project(masked, w_out).astype(jnp.bfloat16)
    grad_groups = grouped(attended_grad, group_width)

    def query_group(parts):
        query_part, key_part, value_part, grad_part, log_part = parts
        weights_half, grad_scores, row_delta = softmax_grads(
            query_part, key_part, value_part, grad_part, log_part, None, allowed, head_size, factor
        )
        key_heads = key_part.reshape(key_part.shape[0], -1, head_size)
        query_grad = (
            jnp.einsum("hqk,khd->qhd", grad_scores, key_heads, preferred_element_type=jnp.float32)
            * factor
        )
        summ_kgrad, summ_vgrad = key_side(
            grad_scores[:, :, near_rows:],
            weights_half[:, :, near_rows:],
            query_part,
            grad_part,
            head_size,
            factor,
        )
        outputs = (query_grad.reshape(query_grad.shape[0], -1), summ_kgrad, summ_vgrad, row_delta)
        outputs = outputs + key_side(
            grad_scores[:, :, :near_rows],
            weights_half[:, :, :near_rows],
            query_part,
            grad_part,
            head_size,
            factor,
        )
        return outputs

    results = lax.map(
        query_group, (query_groups, key_groups, value_groups, grad_groups, log_totals)
    )
    query_grad = ungrouped(results[0]).astype(jnp.bfloat16)
    summary_part = jnp.concatenate([ungrouped(results[1]), ungrouped(results[2])], axis=1)
    row_delta = results[3]
    near_grad = jnp.concatenate([ungrouped(results[4]), ungrouped(results[5])], axis=1).reshape(
        3, 3, tile_rows, 2 * model_width
    )
    from_lower = passed_along(near_grad[:, 2].astype(jnp.bfloat16), "tx", 1).astype(jnp.float32)
    from_upper = passed_along(near_grad[:, 0].astype(jnp.bfloat16), "tx", -1).astype(jnp.float32)
    column_sum = near_grad[:, 1] + from_lower + from_upper
    row_lower = passed_along(shortened(column_sum[2]), "ty", 1)
    row_upper = passed_along(shortened(column_sum[0]), "ty", -1)
    own_grad = column_sum[1] + row_lower + row_upper
    key_grad = own_grad[:, :model_width].astype(jnp.bfloat16)
    value_grad = own_grad[:, model_width:].astype(jnp.bfloat16)
    summary_grad = lax.psum_scatter(summary_part, ("ty", "tx"), scatter_dimension=0, tiled=True)
    summary_key_grad = summary_grad[:, :model_width]
    summary_value_grad = summary_grad[:, model_width:]
    summary_hidden_grad = exact_back(summary_key_grad, w_key) + exact_back(
        summary_value_grad, w_value
    )
    summary_key_proj = exact_rows(summary_hidden, summary_key_grad)
    summary_value_proj = exact_rows(summary_hidden, summary_value_grad)
    hidden_grad = (
        back_project(query_grad, w_query)
        + back_project(key_grad, w_key)
        + back_project(value_grad, w_value)
    )
    weight_part = jnp.stack(
        [
            contract_rows(hidden, query_grad),
            contract_rows(hidden, key_grad) + summary_key_proj,
            contract_rows(hidden, value_grad) + summary_value_proj,
            contract_rows(attended, masked),
        ]
    )
    gain_part = jnp.sum(hidden_grad * token_rows.astype(jnp.float32) * row_scale, axis=0) + jnp.sum(
        summary_hidden_grad * summary.astype(jnp.float32) * summary_scale, axis=0
    )
    grad_proj, grad_gain = lax.psum((weight_part, gain_part), ("ty", "tx"))
    grad_tokens = (
        grads_in.astype(jnp.float32) + norm_back(token_rows, row_scale, norm_gain, hidden_grad)
    ).astype(jnp.bfloat16)
    grad_summary = norm_back(summary, summary_scale, norm_gain, summary_hidden_grad).astype(
        jnp.bfloat16
    )
    return (
        updated.reshape(tokens.shape),
        grad_tokens.reshape(tokens.shape),
        grad_summary,
        grad_proj,
        grad_gain,
    )


def solution(mesh):
    return jax.shard_map(
        local,
        mesh=mesh,
        in_specs=(
            P(("slide", "ty"), "tx", None, None),
            P(("slide", "ty", "tx"), None),
            P("slide", None),
            P("slide", None, None),
            P(("slide", "ty"), "tx", None),
            P(),
            P(),
            P(("slide", "ty"), "tx", None, None),
        ),
        out_specs=(
            P(("slide", "ty"), "tx", None, None),
            P(("slide", "ty"), "tx", None, None),
            P(("slide", "ty", "tx"), None),
            P("slide", None, None),
            P("slide"),
        ),
        check_vma=False,
    )
```

profile of v0, /device:TPU:0, one launch (start us, length us, event | category | flops | bytes accessed | tf_op | source)
XLA Modules:
  0.0 711.2 jit_solution(4504195539969881857)
XLA Ops:
  7.2 1.1 fusion.55
  8.4 1.8 convolution_convert_fusion.4
  10.2 1.8 convolution_convert_fusion.5
  12.1 1.4 collective-permute-start.1
  13.6 5.5 collective-permute-start
  20.8 1.7 convolution_convert_fusion.3
  24.6 1.8 convolution_convert_fusion.2
  27.9 3.5 collective-permute-done.1
  31.9 1.3 collective-permute-start.3
  33.2 4.7 collective-permute-start.2
  38.2 86.2 %all_gather.3 = bf16[256,768]{1,0:T(8,128)(2,1)S(1)} all-gather(bf16[16,768]{1,0:T(8,128)(2,1)S(1)} %fusion.83), channel_id=1, replica_groups=mesh['ty'=4,'tx'=4,'slide'=2] {'ty','tx'}, dimensions={0}, use_global_device_ids=true | all-gather | bytes 417792 | tf_op jit(solution)/shard_map/all_gather | solution.py:150
  124.4 1.7 convolution_convert_fusion.1
  126.1 1.7 convolution_convert_fusion
  129.0 3.1 pad_maximum_fusion.2
  132.1 3.2 copy.29
  135.2 4.6 copy.30
  139.9 28.4 %while.30 = (s32[]{:T(128)}, bf16[6,192,128]{1,2,0:T(8,128)(2,1)}, f32[6,2,192]{2,1,0:T(2,128)S(1)}, bf16[6,1984,128]{1,2,0:T(8,128)(2,1)S(1)}, pred[1984]{0:T(1...) while((s32[]{:T(128)}, bf16[6,192,128]{1,2,0:T(8,128)(2,1)}, ...), condition=%wide.region_5.6_spmd, body=%wide.region_2.5_spmd.sunk | while | flops 201154176 | bytes 12516909 | solution.py:191
  144.6 1.1 constant_dynamic-slice_fusion.14
  149.3 1.1 constant_dynamic-slice_fusion.14
  154.1 1.1 constant_dynamic-slice_fusion.14
  158.8 1.1 constant_dynamic-slice_fusion.14
  168.3 59.4 %while.31 = (s32[]{:T(128)}, bf16[6,192,128]{1,2,0:T(8,128)(2,1)}, f32[6,256,128]{1,2,0:T(8,128)}, f32[6,256,128]{1,2,0:T(8,128)}, f32[6,1728,128]{1,2,0:T(8,128...) while((s32[]{:T(128)}, bf16[6,192,128]{1,2,0:T(8,128)(2,1)}, ...), condition=%wide.region_8.9_spmd, body=%wide.region_6.8_spmd.sunk | while | flops 494747264 | bytes 33400420 | solution.py:228
  171.7 1.2 multiply_reduce_fusion.2
  176.8 1.4 constant_dynamic-update-slice_fusion.15
  181.6 1.2 multiply_reduce_fusion.2
  186.6 1.4 constant_dynamic-update-slice_fusion.15
  191.5 1.2 multiply_reduce_fusion.2
  196.6 1.4 constant_dynamic-update-slice_fusion.15
  201.4 1.2 multiply_reduce_fusion.2
  206.4 1.4 constant_dynamic-update-slice_fusion.15
  211.3 1.2 multiply_reduce_fusion.2
  216.3 1.4 constant_dynamic-update-slice_fusion.15
  221.1 1.2 multiply_reduce_fusion.2
  226.2 1.4 constant_dynamic-update-slice_fusion.15
  227.6 7.5 %copy.34 = f32[1728,6,128]{2,1,0:T(8,128)} copy(f32[1728,6,128]{0,2,1:T(8,128)} %bitcast.284) | data formatting | bytes 10616832 | tf_op jit(solution)/shard_map/transpose | solution.py:84
  235.1 7.1 concatenate.35
  242.2 5.4 constant_dynamic-update-slice_fusion.7
  247.6 7.5 %copy.35 = f32[1728,6,128]{2,1,0:T(8,128)} copy(f32[1728,6,128]{0,2,1:T(8,128)} %bitcast.285) | data formatting | bytes 10616832 | tf_op jit(solution)/shard_map/transpose | solution.py:84
  255.1 7.1 %concatenate.36 = f32[3,3,192,768]{3,2,1,0:T(8,128)} reshape(f32[1728,6,128]{2,1,0:T(8,128)} %copy.35) | data formatting | bytes 10616832 | tf_op jit(solution)/shard_map/concatenate | solution.py:234
  262.2 5.4 constant_dynamic-update-slice_fusion.6
  267.6 4.7 convert.14
  272.4 2.0 slice_bitcast_fusion.2
  274.4 1.3 collective-permute-start.5
  275.7 5.8 collective-permute-start.4
  281.6 1.6 copy.37
  283.5 30.0 %collective-permute-done.5 = bf16[3,192,1536]{2,1,0:T(8,128)(2,1)} collective-permute-done((bf16[3,192,1536]{2,1,0:T(8,128)(2,1)}, bf16[3,192,1536]{2,1,0:T(8,128)(2,1)}, u32[]{:S(2)}, u32[]{:S(2)}) %collective-permute-start.5) | collective-permute-done | bytes 1769504 | tf_op jit(solution)/shard_map/ppermute | solution.py:32
  313.5 2.0 collective-permute-done.4
  315.5 3.9 fusion.102
  319.5 1.4 collective-permute-start.7
  320.9 4.6 collective-permute-start.6
  326.1 2.0 convolution_bitcast_fusion.1
  328.1 4.3 collective-permute-done.7
  333.5 74.2 %reduce-scatter.4.cloned.1.call-done = f32[16,1536]{1,0:T(8,128)} async-done(((f32[256,1536]{1,0:T(8,128)}), f32[16,1536]{1,0:T(8,128)}) %reduce-scatter.4.cloned.1.call-update) | async-done | bytes 98320
  407.6 1.9 fusion.91
  410.5 1.1 fusion.94
  413.2 4.0 pad_maximum_fusion
  418.3 2.6 fusion.32
  420.9 2.1 fusion.19
  423.0 1.9 convolution_add_fusion.1
  424.9 2.0 fusion.64
  428.8 1.2 fusion.89
  430.0 42.8 %psum.15 = f32[768]{0:T(1024)} all-reduce(f32[768]{0:T(1024)S(1)} %add.120), channel_id=1, replica_groups=mesh['ty'=4,'tx'=4,'slide'=2] {'ty','tx'}, use_global_device_ids=true, to_apply=%region_15.16 | all-reduce | flops 768 | bytes 6144 | tf_op jit(solution)/shard_map/psum | solution.py:269
  473.5 222.8 %all-reduce.3.cloned.1.call-done = f32[4,768,768]{2,1,0:T(8,128)} async-done(((f32[4,768,768]{2,1,0:T(8,128)}), f32[4,768,768]{2,1,0:T(8,128)}) %all-reduce.3.cloned.1.call-update) | async-done | bytes 9437200 | tf_op jit(solution)/shard_map/psum | solution.py:269
  696.3 8.0 %copy.80 = f32[4,768,768]{2,1,0:T(8,128)} copy(f32[4,768,768]{2,1,0:T(8,128)} %all-reduce.3.cloned.1.call-done) | data formatting | bytes 18874368
  (209 shorter events, 82.7 us)
Async XLA Ops:
  7.2 13.7 %copy-start.1 = (bf16[1,1,192,768]{3,2,1,0:T(8,128)(2,1)S(1)}, bf16[1,1,192,768]{3,2,1,0:T(8,128)(2,1)}, u32[]{:S(2)}) copy-start(bf16[1,1,192,768]{3,2,1,0:T(8,128)(2,1)} %param.12) | copy-start | bytes 884740
  7.2 13.7 %copy-start.13 = (f32[768]{0:T(1024)S(1)}, f32[768]{0:T(1024)}, u32[]{:S(2)}) copy-start(f32[768]{0:T(1024)} %param.17) | copy-start | bytes 9220
  7.2 12.0 %copy-start.14 = (s32[4,4]{1,0:T(4,128)S(1)}, s32[4,4]{1,0:T(4,128)}, u32[]{:S(2)}) copy-start(s32[4,4]{1,0:T(4,128)} %param.14) | copy-start | bytes 196
  7.2 400.4 %reduce-scatter.4.cloned.1.call-start = ((), (), s32[]{:S(2)}) async-start(), calls=%async_computation.2 | async-start | bytes 1671168
  12.1 12.5 %copy-start.4 = (bf16[1,1,192,768]{3,2,1,0:T(8,128)(2,1)S(1)}, bf16[1,1,192,768]{3,2,1,0:T(8,128)(2,1)}, u32[]{:S(2)}) copy-start(bf16[1,1,192,768]{3,2,1,0:T(8,128)(2,1)} %param.19) | copy-start | bytes 884740
  12.1 19.2 %collective-permute-start.1 = (bf16[1,1,192,1536]{3,2,1,0:T(8,128)(2,1)S(1)}, bf16[1,1,192,1536]{3,2,1,0:T(8,128)(2,1)S(1)}, u32[]{:S(2)}, u32[]{:S(2)}) collective-permute-start(bf16[1,1,192,1536]{3,2,1,0:T(8,128)(2,1)S(1)} %maximum_bitcast_fusion), channel_id=1, source_target_pairs={{8,0},{16,8},{24,16},{9,1},{17,9},{25,17},{10,2},{18,10},{26,18},{... | collective-permute-start | bytes 1769480 | tf_op jit(solution)/shard_map/ppermute | solution.py:22
  13.6 18.1 %collective-permute-start = (bf16[1,1,192,1536]{3,2,1,0:T(8,128)(2,1)S(1)}, bf16[1,1,192,1536]{3,2,1,0:T(8,128)(2,1)S(1)}, u32[]{:S(2)}, u32[]{:S(2)}) collective-permute-start(bf16[1,1,192,1536]{3,2,1,0:T(8,128)(2,1)S(1)} %maximum_bitcast_fusion), channel_id=1, source_target_pairs={{0,8},{8,16},{16,24},{1,9},{9,17},{17,25},{2,10},{10,18},{18,26},{... | collective-permute-start | bytes 1769480 | tf_op jit(solution)/shard_map/ppermute | solution.py:20
  24.6 13.2 %copy-start.15 = (s32[1,1,2]{2,1,0:T(1,128)S(1)}, s32[1,1,2]{2,1,0:T(1,128)}, u32[]{:S(2)}) copy-start(s32[1,1,2]{2,1,0:T(1,128)} %param.16) | copy-start | bytes 28
  24.6 13.4 %copy-start.12 = (bf16[16,768]{1,0:T(8,128)(2,1)S(1)}, bf16[16,768]{1,0:T(8,128)(2,1)}, u32[]{:S(2)}) copy-start(bf16[16,768]{1,0:T(8,128)(2,1)} %param.13) | copy-start | bytes 73732
  31.9 96.1 %collective-permute-start.3 = (bf16[3,1,192,1536]{3,2,1,0:T(8,128)(2,1)S(1)}, bf16[3,1,192,1536]{3,2,1,0:T(8,128)(2,1)S(1)}, u32[]{:S(2)}, u32[]{:S(2)}) collective-permute-start(bf16[3,1,192,1536]{3,2,1,0:T(8,128)(2,1)S(1)} %pad_maximum_fusion.4), channel_id=1, source_target_pairs={{2,0},{4,2},{6,4},{3,1},{5,3},{7,5},{10,8},{12,10},{14,12},{11,9},... | collective-permute-start | bytes 5308424 | tf_op jit(solution)/shard_map/ppermute | solution.py:22
  33.2 94.8 %collective-permute-start.2 = (bf16[3,1,192,1536]{3,2,1,0:T(8,128)(2,1)S(1)}, bf16[3,1,192,1536]{3,2,1,0:T(8,128)(2,1)S(1)}, u32[]{:S(2)}, u32[]{:S(2)}) collective-permute-start(bf16[3,1,192,1536]{3,2,1,0:T(8,128)(2,1)S(1)} %pad_maximum_fusion.4), channel_id=1, source_target_pairs={{0,2},{2,4},{4,6},{1,3},{3,5},{5,7},{8,10},{10,12},{12,14},{9,11},... | collective-permute-start | bytes 5308424 | tf_op jit(solution)/shard_map/ppermute | solution.py:20
  272.4 9.2 %copy-start.7 = (f32[6,256,128]{1,2,0:T(8,128)S(1)}, f32[6,256,128]{1,2,0:T(8,128)}, u32[]{:S(2)}) copy-start(f32[6,256,128]{1,2,0:T(8,128)} %get-tuple-element.114) | copy-start | bytes 2359300
  272.4 9.1 %copy-start.8 = (f32[6,256,128]{1,2,0:T(8,128)S(1)}, f32[6,256,128]{1,2,0:T(8,128)}, u32[]{:S(2)}) copy-start(f32[6,256,128]{1,2,0:T(8,128)} %get-tuple-element.115) | copy-start | bytes 2359300
  274.4 39.1 %collective-permute-start.5 = (bf16[3,192,1536]{2,1,0:T(8,128)(2,1)}, bf16[3,192,1536]{2,1,0:T(8,128)(2,1)}, u32[]{:S(2)}, u32[]{:S(2)}) collective-permute-start(bf16[3,192,1536]{2,1,0:T(8,128)(2,1)} %get-tuple-element.211), channel_id=1, source_target_pairs={{2,0},{4,2},{6,4},{3,1},{5,3},{7,5},{10,8},{12,10},{14,12},{11,9},... | collective-permute-start | bytes 5308424 | tf_op jit(solution)/shard_map/ppermute | solution.py:32
  275.7 39.8 %collective-permute-start.4 = (bf16[3,192,1536]{2,1,0:T(8,128)(2,1)}, bf16[3,192,1536]{2,1,0:T(8,128)(2,1)}, u32[]{:S(2)}, u32[]{:S(2)}) collective-permute-start(bf16[3,192,1536]{2,1,0:T(8,128)(2,1)} %get-tuple-element.210), channel_id=1, source_target_pairs={{0,2},{2,4},{4,6},{1,3},{3,5},{5,7},{8,10},{10,12},{12,14},{9,11},... | collective-permute-start | bytes 5308424 | tf_op jit(solution)/shard_map/ppermute | solution.py:32
  283.2 42.3 %copy-start.5 = (bf16[1,1,192,768]{3,2,1,0:T(8,128)(2,1)S(1)}, bf16[1,1,192,768]{3,2,1,0:T(8,128)(2,1)}, u32[]{:S(2)}) copy-start(bf16[1,1,192,768]{3,2,1,0:T(8,128)(2,1)} %param.19) | copy-start | bytes 884740
  283.3 413.1 %all-reduce.3.cloned.1.call-start = ((), (), s32[]{:S(2)}) async-start(), calls=%async_computation.1 | async-start | bytes 18874368 | tf_op jit(solution)/shard_map/psum | solution.py:269
  283.5 42.0 %copy-start.9 = (bf16[6,192,128]{1,2,0:T(8,128)(2,1)S(1)}, bf16[6,192,128]{1,2,0:T(8,128)(2,1)}, u32[]{:S(2)}) copy-start(bf16[6,192,128]{1,2,0:T(8,128)(2,1)} %get-tuple-element.109) | copy-start | bytes 884740
  319.4 6.7 copy-start.2
  319.5 12.9 %collective-permute-start.7 = (bf16[192,1536]{1,0:T(8,128)(2,1)S(1)}, bf16[192,1536]{1,0:T(8,128)(2,1)S(1)}, u32[]{:S(2)}, u32[]{:S(2)}) collective-permute-start(bf16[192,1536]{1,0:T(8,128)(2,1)S(1)} %get-tuple-element.215), channel_id=1, source_target_pairs={{8,0},{16,8},{24,16},{9,1},{17,9},{25,17},{10,2},{18,10},{26,18},{... | collective-permute-start | bytes 1769480 | tf_op jit(solution)/shard_map/ppermute | solution.py:32
  320.9 12.3 %collective-permute-start.6 = (bf16[192,1536]{1,0:T(8,128)(2,1)S(1)}, bf16[192,1536]{1,0:T(8,128)(2,1)S(1)}, u32[]{:S(2)}, u32[]{:S(2)}) collective-permute-start(bf16[192,1536]{1,0:T(8,128)(2,1)S(1)} %get-tuple-element.214), channel_id=1, source_target_pairs={{0,8},{8,16},{16,24},{1,9},{9,17},{17,25},{2,10},{10,18},{18,26},{... | collective-permute-start | bytes 1769480 | tf_op jit(solution)/shard_map/ppermute | solution.py:32
  409.6 0.9 copy-start.11
  411.6 1.7 copy-start
  417.3 1.0 copy-start.10
  417.3 3.6 copy-start.3
  417.3 10.5 %slice-start = ((s8[4718592]{0:T(1024)(128)(4,1)}), s8[524288]{0:T(1024)(128)(4,1)S(1)}, s32[]{:S(2)}) async-start(s8[4718592]{0:T(1024)(128)(4,1)} %bitcast.286), calls=%async_computation.3 | async-start | bytes 1048576
  418.3 9.5 %slice-start.1 = ((s8[4718592]{0:T(1024)(128)(4,1)}), s8[4194304]{0:T(1024)(128)(4,1)S(1)}, s32[]{:S(2)}) async-start(s8[4718592]{0:T(1024)(128)(4,1)} %bitcast.286), calls=%async_computation.4 | async-start | bytes 8388608
  422.9 3.9 copy-start.6
Sparse Core Ops, SparseCore 0:
  283.4 124.2 reduce-scatter.3
  417.4 278.8 all-reduce.2
where the time goes:
time: 714 us; the launch traced here: 711 us
  waiting for transfers between devices  338 us (47%)
  blocking collectives  129 us (18%)
  local copies, waits for them, and re-layouts  114 us (16%)
  matrix products  59.7 us (8%)
  other arithmetic  29.2 us (4%)
  starting transfers between devices  26.3 us (4%)
  between operations  14.6 us (2%)
    psum x1, waiting for transfers between devices, local(): grad_proj, grad_gain = lax.psum((weight_part, gain_part), ('ty', 'tx'))  223 us
    all_gather x1, blocking collectives, local(): piece = lax.all_gather(summary_hidden, ('ty', 'tx'), axis=0, tiled=True)  86.2 us
    unnamed x3, waiting for transfers between devices  74.2 us
    psum x1, blocking collectives, local(): grad_proj, grad_gain = lax.psum((weight_part, gain_part), ('ty', 'tx'))  42.8 us
    ppermute x4, waiting for transfers between devices, passed_along(): return lax.ppermute(array, axis, pairs)  37.1 us
    dynamic_slice x36, local copies, waits for them, and re-layouts, local(): lax.map(forward_group, (query_groups, key_groups, value_groups))  28.7 us
    concatenate x3, local copies, waits for them, and re-layouts, local(): jnp.concatenate([ungrouped(results[4]), ungrouped(results[5])], axis=1)  19.6 us
    unnamed x39, local copies, waits for them, and re-layouts  16.6 us
  transfers between devices with their start and end apart: 10, of which 8 were waited for; matrix products, arithmetic and copies ran while one was open for 5% of the time, Pallas kernels for 0%

commit v1 on v0

--- a/solution.py
+++ b/solution.py
@@ -266,7 +266,7 @@
     gain_part = jnp.sum(hidden_grad * token_rows.astype(jnp.float32) * row_scale, axis=0) + jnp.sum(
         summary_hidden_grad * summary.astype(jnp.float32) * summary_scale, axis=0
     )
-    grad_proj, grad_gain = lax.psum((weight_part, gain_part), ("ty", "tx"))
+    grad_proj, grad_gain = lax.psum(lax.psum((weight_part, gain_part), "tx"), "ty")
     grad_tokens = (
         grads_in.astype(jnp.float32) + norm_back(token_rows, row_scale, norm_gain, hidden_grad)
     ).astype(jnp.bfloat16)

time: 714 us -> 951 us (1.33)
  waiting for transfers between devices: 338 us -> 596 us
  blocking collectives: 129 us -> 106 us
    psum x1 -> x2, waiting for transfers between devices: 223 us -> 481 us  [the longest x1 324 us: local(): lax.psum((weight_part, gain_part), 'tx')]
    psum x1 -> x2, blocking collectives: 42.8 us -> 20.2 us  [the longest x1 11.1 us: local(): lax.psum(lax.psum((weight_part, gain_part), 'tx'), 'ty')]
    unnamed x3 -> x4, waiting for transfers between devices: 74.2 us -> 74.3 us
  transfers between devices with their start and end apart: 10 -> 11, of which waited for: 8 -> 9; matrix products, arithmetic and copies ran while one was open for 5% -> 4% of each run, Pallas kernels for 0% -> 0%
where the time goes in v1:
time: 951 us; the launch traced here: 948 us
  waiting for transfers between devices  596 us (63%)
  local copies, waits for them, and re-layouts  114 us (12%)
  blocking collectives  106 us (11%)
  matrix products  59.8 us (6%)
  other arithmetic  29.7 us (3%)
  starting transfers between devices  26.3 us (3%)
  between operations  14.3 us (2%)
    psum x1, waiting for transfers between devices, local(): lax.psum((weight_part, gain_part), 'tx')  324 us
    psum x1, waiting for transfers between devices, local(): lax.psum(lax.psum((weight_part, gain_part), 'tx'), 'ty')  157 us
    all_gather x1, blocking collectives, local(): piece = lax.all_gather(summary_hidden, ('ty', 'tx'), axis=0, tiled=True)  86.2 us
    unnamed x4, waiting for transfers between devices  74.3 us
    ppermute x4, waiting for transfers between devices, passed_along(): return lax.ppermute(array, axis, pairs)  37.1 us
    dynamic_slice x36, local copies, waits for them, and re-layouts, local(): lax.map(forward_group, (query_groups, key_groups, value_groups))  28.7 us
    concatenate x3, local copies, waits for them, and re-layouts, local(): jnp.concatenate([ungrouped(results[4]), ungrouped(results[5])], axis=1)  19.7 us
  transfers between devices with their start and end apart: 11, of which 9 were waited for; matrix products, arithmetic and copies ran while one was open for 4% of the time, Pallas kernels for 0%

profile of v1, /device:TPU:0, one launch (start us, length us, event | category | flops | bytes accessed | tf_op | source)
XLA Modules:
  0.0 947.5 jit_solution(2658482670735750148)
XLA Ops:
  7.2 1.1 fusion.55
  9.0 1.8 convolution_convert_fusion.4
  10.8 1.8 convolution_convert_fusion.5
  12.7 1.4 collective-permute-start.1
  14.1 5.5 collective-permute-start
  21.4 1.7 convolution_convert_fusion.3
  25.2 1.8 convolution_convert_fusion.2
  28.4 3.5 collective-permute-done.1
  32.4 1.3 collective-permute-start.3
  33.7 4.7 collective-permute-start.2
  38.8 86.2 %all_gather.3 = bf16[256,768]{1,0:T(8,128)(2,1)S(1)} all-gather(bf16[16,768]{1,0:T(8,128)(2,1)S(1)} %fusion.83), channel_id=1, replica_groups=mesh['ty'=4,'tx'=4,'slide'=2] {'ty','tx'}, dimensions={0}, use_global_device_ids=true | all-gather | bytes 417792 | tf_op jit(solution)/shard_map/all_gather | solution.py:150
  125.0 1.7 convolution_convert_fusion.1
  126.7 1.7 convolution_convert_fusion
  129.5 3.0 pad_maximum_fusion.2
  132.6 3.2 copy.29
  135.7 4.6 copy.30
  140.4 28.4 %while.30 = (s32[]{:T(128)}, bf16[6,192,128]{1,2,0:T(8,128)(2,1)}, f32[6,2,192]{2,1,0:T(2,128)S(1)}, bf16[6,1984,128]{1,2,0:T(8,128)(2,1)S(1)}, pred[1984]{0:T(1...) while((s32[]{:T(128)}, bf16[6,192,128]{1,2,0:T(8,128)(2,1)}, ...), condition=%wide.region_5.6_spmd, body=%wide.region_2.5_spmd.sunk | while | flops 201154176 | bytes 12516909 | solution.py:191
  145.1 1.1 constant_dynamic-slice_fusion.14
  154.6 1.1 constant_dynamic-slice_fusion.14
  168.8 59.4 %while.31 = (s32[]{:T(128)}, bf16[6,192,128]{1,2,0:T(8,128)(2,1)}, f32[6,256,128]{1,2,0:T(8,128)}, f32[6,256,128]{1,2,0:T(8,128)}, f32[6,1728,128]{1,2,0:T(8,128...) while((s32[]{:T(128)}, bf16[6,192,128]{1,2,0:T(8,128)(2,1)}, ...), condition=%wide.region_8.9_spmd, body=%wide.region_6.8_spmd.sunk | while | flops 494747264 | bytes 33400420 | solution.py:228
  172.3 1.2 multiply_reduce_fusion.2
  177.3 1.4 constant_dynamic-update-slice_fusion.15
  182.1 1.2 multiply_reduce_fusion.2
  187.2 1.4 constant_dynamic-update-slice_fusion.15
  192.0 1.2 multiply_reduce_fusion.2
  197.1 1.4 constant_dynamic-update-slice_fusion.15
  201.9 1.2 multiply_reduce_fusion.2
  207.0 1.4 constant_dynamic-update-slice_fusion.15
  211.8 1.2 multiply_reduce_fusion.2
  216.8 1.4 constant_dynamic-update-slice_fusion.15
  221.7 1.2 multiply_reduce_fusion.2
  226.7 1.4 constant_dynamic-update-slice_fusion.15
  228.2 7.5 copy.34
  235.7 7.1 concatenate.35
  242.8 5.4 constant_dynamic-update-slice_fusion.7
  248.1 7.5 copy.35
  255.7 7.1 concatenate.36
  262.8 5.5 constant_dynamic-update-slice_fusion.6
  268.2 4.7 convert.14
  273.0 2.0 slice_bitcast_fusion.2
  275.0 1.3 collective-permute-start.5
  276.3 5.8 collective-permute-start.4
  282.2 1.6 copy.37
  284.1 30.0 %collective-permute-done.5 = bf16[3,192,1536]{2,1,0:T(8,128)(2,1)} collective-permute-done((bf16[3,192,1536]{2,1,0:T(8,128)(2,1)}, bf16[3,192,1536]{2,1,0:T(8,128)(2,1)}, u32[]{:S(2)}, u32[]{:S(2)}) %collective-permute-start.5) | collective-permute-done | bytes 1769504 | tf_op jit(solution)/shard_map/ppermute | solution.py:32
  314.1 2.0 collective-permute-done.4
  316.1 3.9 fusion.102
  320.1 1.4 collective-permute-start.7
  321.5 4.6 collective-permute-start.6
  326.7 2.0 convolution_bitcast_fusion.1
  328.7 4.3 collective-permute-done.7
  334.1 74.2 %reduce-scatter.4.cloned.1.call-done = f32[16,1536]{1,0:T(8,128)} async-done(((f32[256,1536]{1,0:T(8,128)}), f32[16,1536]{1,0:T(8,128)}) %reduce-scatter.4.cloned.1.call-update) | async-done | bytes 98320
  408.3 1.9 fusion.91
  411.1 1.1 fusion.94
  413.9 4.0 pad_maximum_fusion
  418.0 323.7 %all-reduce.4.cloned.1.call-done = f32[4,768,768]{2,1,0:T(8,128)} async-done(((f32[4,768,768]{2,1,0:T(8,128)}), f32[4,768,768]{2,1,0:T(8,128)}) %all-reduce.4.cloned.1.call-update) | async-done | bytes 9437200 | tf_op jit(solution)/shard_map/psum | solution.py:269
  742.8 2.6 fusion.32
  745.3 1.8 fusion.19
  747.2 1.9 convolution_add_fusion.1
  749.0 2.3 fusion.64
  753.4 1.2 fusion.89
  754.6 9.1 psum.30
  763.7 11.1 %psum.31 = f32[768]{0:T(1024)} all-reduce(f32[768]{0:T(1024)S(1)} %psum.30), channel_id=1, replica_groups=mesh['ty'=4,'tx'=4,'slide'=2] {'ty'}, use_global_device_ids=true, to_apply=%region_17.18 | all-reduce | flops 768 | bytes 6144 | tf_op jit(solution)/shard_map/psum | solution.py:269
  775.5 157.5 %all-reduce.6.cloned.1.call-done = f32[4,768,768]{2,1,0:T(8,128)} async-done(((f32[4,768,768]{2,1,0:T(8,128)}), f32[4,768,768]{2,1,0:T(8,128)}) %all-reduce.6.cloned.1.call-update) | async-done | bytes 9437200 | tf_op jit(solution)/shard_map/psum | solution.py:269
  933.0 8.0 copy.81
  (215 shorter events, 85.6 us)
Async XLA Ops:
  7.2 14.2 %copy-start.1 = (bf16[1,1,192,768]{3,2,1,0:T(8,128)(2,1)S(1)}, bf16[1,1,192,768]{3,2,1,0:T(8,128)(2,1)}, u32[]{:S(2)}) copy-start(bf16[1,1,192,768]{3,2,1,0:T(8,128)(2,1)} %param.12) | copy-start | bytes 884740
  7.2 14.2 %copy-start.13 = (f32[768]{0:T(1024)S(1)}, f32[768]{0:T(1024)}, u32[]{:S(2)}) copy-start(f32[768]{0:T(1024)} %param.17) | copy-start | bytes 9220
  7.2 12.6 %copy-start.15 = (s32[4,4]{1,0:T(4,128)S(1)}, s32[4,4]{1,0:T(4,128)}, u32[]{:S(2)}) copy-start(s32[4,4]{1,0:T(4,128)} %param.14) | copy-start | bytes 196
  7.2 401.1 %reduce-scatter.4.cloned.1.call-start = ((), (), s32[]{:S(2)}) async-start(), calls=%async_computation.3 | async-start | bytes 1671168
  12.6 12.5 %copy-start.4 = (bf16[1,1,192,768]{3,2,1,0:T(8,128)(2,1)S(1)}, bf16[1,1,192,768]{3,2,1,0:T(8,128)(2,1)}, u32[]{:S(2)}) copy-start(bf16[1,1,192,768]{3,2,1,0:T(8,128)(2,1)} %param.19) | copy-start | bytes 884740
  12.7 19.2 %collective-permute-start.1 = (bf16[1,1,192,1536]{3,2,1,0:T(8,128)(2,1)S(1)}, bf16[1,1,192,1536]{3,2,1,0:T(8,128)(2,1)S(1)}, u32[]{:S(2)}, u32[]{:S(2)}) collective-permute-start(bf16[1,1,192,1536]{3,2,1,0:T(8,128)(2,1)S(1)} %maximum_bitcast_fusion), channel_id=1, source_target_pairs={{8,0},{16,8},{24,16},{9,1},{17,9},{25,17},{10,2},{18,10},{26,18},{... | collective-permute-start | bytes 1769480 | tf_op jit(solution)/shard_map/ppermute | solution.py:22
  14.1 18.1 %collective-permute-start = (bf16[1,1,192,1536]{3,2,1,0:T(8,128)(2,1)S(1)}, bf16[1,1,192,1536]{3,2,1,0:T(8,128)(2,1)S(1)}, u32[]{:S(2)}, u32[]{:S(2)}) collective-permute-start(bf16[1,1,192,1536]{3,2,1,0:T(8,128)(2,1)S(1)} %maximum_bitcast_fusion), channel_id=1, source_target_pairs={{0,8},{8,16},{16,24},{1,9},{9,17},{17,25},{2,10},{10,18},{18,26},{... | collective-permute-start | bytes 1769480 | tf_op jit(solution)/shard_map/ppermute | solution.py:20
  25.2 13.2 %copy-start.16 = (s32[1,1,2]{2,1,0:T(1,128)S(1)}, s32[1,1,2]{2,1,0:T(1,128)}, u32[]{:S(2)}) copy-start(s32[1,1,2]{2,1,0:T(1,128)} %param.16) | copy-start | bytes 28
  25.2 13.4 %copy-start.12 = (bf16[16,768]{1,0:T(8,128)(2,1)S(1)}, bf16[16,768]{1,0:T(8,128)(2,1)}, u32[]{:S(2)}) copy-start(bf16[16,768]{1,0:T(8,128)(2,1)} %param.13) | copy-start | bytes 73732
  32.4 96.1 %collective-permute-start.3 = (bf16[3,1,192,1536]{3,2,1,0:T(8,128)(2,1)S(1)}, bf16[3,1,192,1536]{3,2,1,0:T(8,128)(2,1)S(1)}, u32[]{:S(2)}, u32[]{:S(2)}) collective-permute-start(bf16[3,1,192,1536]{3,2,1,0:T(8,128)(2,1)S(1)} %pad_maximum_fusion.4), channel_id=1, source_target_pairs={{2,0},{4,2},{6,4},{3,1},{5,3},{7,5},{10,8},{12,10},{14,12},{11,9},... | collective-permute-start | bytes 5308424 | tf_op jit(solution)/shard_map/ppermute | solution.py:22
  33.7 94.8 %collective-permute-start.2 = (bf16[3,1,192,1536]{3,2,1,0:T(8,128)(2,1)S(1)}, bf16[3,1,192,1536]{3,2,1,0:T(8,128)(2,1)S(1)}, u32[]{:S(2)}, u32[]{:S(2)}) collective-permute-start(bf16[3,1,192,1536]{3,2,1,0:T(8,128)(2,1)S(1)} %pad_maximum_fusion.4), channel_id=1, source_target_pairs={{0,2},{2,4},{4,6},{1,3},{3,5},{5,7},{8,10},{10,12},{12,14},{9,11},... | collective-permute-start | bytes 5308424 | tf_op jit(solution)/shard_map/ppermute | solution.py:20
  273.0 9.1 copy-start.7
  273.0 9.1 copy-start.8
  275.0 39.1 %collective-permute-start.5 = (bf16[3,192,1536]{2,1,0:T(8,128)(2,1)}, bf16[3,192,1536]{2,1,0:T(8,128)(2,1)}, u32[]{:S(2)}, u32[]{:S(2)}) collective-permute-start(bf16[3,192,1536]{2,1,0:T(8,128)(2,1)} %get-tuple-element.211), channel_id=1, source_target_pairs={{2,0},{4,2},{6,4},{3,1},{5,3},{7,5},{10,8},{12,10},{14,12},{11,9},... | collective-permute-start | bytes 5308424 | tf_op jit(solution)/shard_map/ppermute | solution.py:32
  276.3 39.8 %collective-permute-start.4 = (bf16[3,192,1536]{2,1,0:T(8,128)(2,1)}, bf16[3,192,1536]{2,1,0:T(8,128)(2,1)}, u32[]{:S(2)}, u32[]{:S(2)}) collective-permute-start(bf16[3,192,1536]{2,1,0:T(8,128)(2,1)} %get-tuple-element.210), channel_id=1, source_target_pairs={{0,2},{2,4},{4,6},{1,3},{3,5},{5,7},{8,10},{10,12},{12,14},{9,11},... | collective-permute-start | bytes 5308424 | tf_op jit(solution)/shard_map/ppermute | solution.py:32
  283.8 42.3 %copy-start.5 = (bf16[1,1,192,768]{3,2,1,0:T(8,128)(2,1)S(1)}, bf16[1,1,192,768]{3,2,1,0:T(8,128)(2,1)}, u32[]{:S(2)}) copy-start(bf16[1,1,192,768]{3,2,1,0:T(8,128)(2,1)} %param.19) | copy-start | bytes 884740
  283.9 457.9 %all-reduce.4.cloned.1.call-start = ((), (), s32[]{:S(2)}) async-start(), calls=%async_computation.1 | async-start | bytes 18874368 | tf_op jit(solution)/shard_map/psum | solution.py:269
  284.1 42.0 %copy-start.9 = (bf16[6,192,128]{1,2,0:T(8,128)(2,1)S(1)}, bf16[6,192,128]{1,2,0:T(8,128)(2,1)}, u32[]{:S(2)}) copy-start(bf16[6,192,128]{1,2,0:T(8,128)(2,1)} %get-tuple-element.109) | copy-start | bytes 884740
  320.0 6.7 copy-start.2
  320.1 12.9 %collective-permute-start.7 = (bf16[192,1536]{1,0:T(8,128)(2,1)S(1)}, bf16[192,1536]{1,0:T(8,128)(2,1)S(1)}, u32[]{:S(2)}, u32[]{:S(2)}) collective-permute-start(bf16[192,1536]{1,0:T(8,128)(2,1)S(1)} %get-tuple-element.215), channel_id=1, source_target_pairs={{8,0},{16,8},{24,16},{9,1},{17,9},{25,17},{10,2},{18,10},{26,18},{... | collective-permute-start | bytes 1769480 | tf_op jit(solution)/shard_map/ppermute | solution.py:32
  321.5 12.3 %collective-permute-start.6 = (bf16[192,1536]{1,0:T(8,128)(2,1)S(1)}, bf16[192,1536]{1,0:T(8,128)(2,1)S(1)}, u32[]{:S(2)}, u32[]{:S(2)}) collective-permute-start(bf16[192,1536]{1,0:T(8,128)(2,1)S(1)} %get-tuple-element.214), channel_id=1, source_target_pairs={{0,8},{8,16},{16,24},{1,9},{9,17},{17,25},{2,10},{10,18},{18,26},{... | collective-permute-start | bytes 1769480 | tf_op jit(solution)/shard_map/ppermute | solution.py:32
  410.2 0.9 copy-start.11
  412.3 1.7 copy-start
  418.0 515.0 %all-reduce.6.cloned.1.call-start = ((), (), s32[]{:S(2)}) async-start(), calls=%async_computation.2 | async-start | bytes 18874368 | tf_op jit(solution)/shard_map/psum | solution.py:269
  741.8 1.0 copy-start.10
  741.8 3.6 copy-start.3
  741.8 10.6 %slice-start = ((s8[4718592]{0:T(1024)(128)(4,1)}), s8[524288]{0:T(1024)(128)(4,1)S(1)}, s32[]{:S(2)}) async-start(s8[4718592]{0:T(1024)(128)(4,1)} %bitcast.286), calls=%async_computation.4 | async-start | bytes 1048576
  742.8 9.6 %slice-start.1 = ((s8[4718592]{0:T(1024)(128)(4,1)}), s8[4194304]{0:T(1024)(128)(4,1)S(1)}, s32[]{:S(2)}) async-start(s8[4718592]{0:T(1024)(128)(4,1)} %bitcast.286), calls=%async_computation.5 | async-start | bytes 8388608
  747.2 4.2 copy-start.6
  747.2 4.2 copy-start.14
Sparse Core Ops, SparseCore 0:
  284.0 124.2 reduce-scatter.3
  418.1 323.6 all-reduce.3
  745.3 187.6 all-reduce.5
